TPU v7x, 32 devices: a whole 2x2x4 slice. The times are simulated.
32 devices in a mesh: ctx: 8 (over z, x), head: 4 (over y, core).
Axes of the slice: x: 2, y: 2, z: 4, core: 2. Of those that a mesh axis runs over, the one named last changes fastest.
Arguments:
- video_rows: bfloat16 [4096, 5120], P('ctx'), may hold values from -6 to 6
- w_query: bfloat16 [5120, 5120], P('ctx', 'head'), may hold values from -0.078125 to 0.078125
- w_output: bfloat16 [5120, 5120], P('ctx', 'head'), may hold values from -0.078125 to 0.078125
- audio_tokens: bfloat16 [2, 32, 768], P(None, 'ctx'), may hold values from -544 to 544
- w_key: bfloat16 [768, 5120], P(None, 'head'), may hold values from -0.21875 to 0.21875
- w_value: bfloat16 [768, 5120], P(None, 'head'), may hold values from -0.21875 to 0.21875
- row_lists: int32 [2, 4096], P(None, 'ctx'), may hold values from 0 to 511, as said below
- row_counts: int32 [2, 8], P(None, 'ctx'), may hold values from 0 to 512, as said below
Outputs:
- layer_out: bfloat16 [4096, 5120], P('ctx', 'head')
Inputs may be any that keep to these rules, and one draw needn't show every extreme that they name: `row_lists`: the first row_counts[s, c] entries of speaker s's block on shard c are distinct, live entries of the two speakers on one shard are distinct rows, and the other entries are arbitrary row numbers of the shard. `row_counts`: on each shard the two counts add up to at most 512.
All inputs are finite; a program needn't handle non-finite values.
Results may differ from a plain program's by a relative error of at most 0.0045.
The roundings to bfloat16 on the way count: a program that leaves them out, or rounds other values in their place, can miss the bound.
Values may be sent and summed in bfloat16 or wider, within the bound.
No kernel may reach another device: no remote copies, remote signals or barrier semaphores. Data moves between devices by JAX's collectives and lax.ppermute only.
A program may use at most 128 MiB of HBM per device.

v0:
```python
import jax
import jax.numpy as jnp
from jax import lax
from jax.sharding import PartitionSpec as P

HD = 128
SPK = 2


def add_rows(left_rows, shard_piece):
    return jnp.dot(left_rows, shard_piece, preferred_element_type=jnp.float32)


def shards(video_rows, w_query, w_output, audio_tokens, w_key, w_value, row_lists, row_counts):
    rows_dev = video_rows.shape[0]
    columns = w_query.shape[1]
    heads_dev = columns // HD
    queries = add_rows(video_rows, lax.all_gather(w_query, "ctx", axis=0, tiled=True)).astype(
        jnp.bfloat16
    )
    whole_audio = lax.all_gather(audio_tokens, "ctx", axis=1, tiled=True)
    key_rows = jnp.einsum(
        "sta,ad->std", whole_audio, w_key, preferred_element_type=jnp.float32
    ).astype(jnp.bfloat16)
    value_rows = jnp.einsum(
        "sta,ad->std", whole_audio, w_value, preferred_element_type=jnp.float32
    ).astype(jnp.bfloat16)
    audio_length = key_rows.shape[1]
    position = jnp.arange(rows_dev, dtype=jnp.int32)
    score_scale = 1.0 / HD**0.5
    summed = jnp.zeros((rows_dev, columns), jnp.float32)
    for speaker in range(SPK):
        target = row_lists[speaker]
        row_live = position < row_counts[speaker, 0]
        picked = queries[target].reshape(rows_dev, heads_dev, HD)
        key_block = key_rows[speaker].reshape(audio_length, heads_dev, HD)
        value_block = value_rows[speaker].reshape(audio_length, heads_dev, HD)
        scores = (
            jnp.einsum("rhd,khd->hrk", picked, key_block, preferred_element_type=jnp.float32)
            * score_scale
        )
        scores = scores - jnp.max(scores, axis=-1, keepdims=True)
        weights = jnp.exp(scores)
        weights = (weights / jnp.sum(weights, axis=-1, keepdims=True)).astype(jnp.bfloat16)
        blended = jnp.einsum(
            "hrk,khd->rhd", weights, value_block, preferred_element_type=jnp.float32
        ).astype(jnp.bfloat16)
        blended = blended.reshape(rows_dev, columns).astype(jnp.float32)
        blended = jnp.where(row_live[:, None], blended, jnp.zeros_like(blended))
        summed = summed.at[target].add(blended)
    attended = summed.astype(jnp.bfloat16)
    all_heads = lax.all_gather(attended, "head", axis=1, tiled=True)
    result = add_rows(all_heads, lax.all_gather(w_output, "ctx", axis=0, tiled=True))
    return result.astype(jnp.bfloat16)


def solution(mesh):
    in_specs = (
        P("ctx", None),
        P("ctx", "head"),
        P("ctx", "head"),
        P(None, "ctx", None),
        P(None, "head"),
        P(None, "head"),
        P(None, "ctx"),
        P(None, "ctx"),
    )
    out_specs = P("ctx", "head")
    return jax.shard_map(shards, mesh=mesh, in_specs=in_specs, out_specs=out_specs, check_vma=False)
```

profile of v0, /device:TPU:0, one launch (start us, length us, event | category | flops | bytes accessed | tf_op | source)
XLA Modules:
  0.0 439.1 jit_solution(14626335249302658859)
XLA Ops:
  6.5 0.0 copy-start
  6.5 0.0 copy-start.3
  6.5 0.0 all-gather.4.cloned.1.call-start
  6.5 0.7 all-gather.4.cloned.1.call-update
  7.3 0.0 all-gather.8.cloned.1.call-start
  7.3 0.7 all-gather.8.cloned.1.call-update
  8.0 0.0 all-gather.6.cloned.1.call-start
  8.1 0.0 copy-done.3
  8.1 32.9 %all_gather.12 = bf16[2,32,768]{2,0,1:T(2,128)(2,1)S(1)} all-gather(bf16[2,4,768]{2,0,1:T(2,128)(2,1)S(1)} %copy.25), channel_id=1, replica_groups=mesh['ctx'=8,'head'=4] {'ctx'}, dimensions={1}, use_global_device_ids=true | all-gather | bytes 110592 | tf_op jit(solution)/shard_map/all_gather | solution.py:21
  41.0 0.0 copy-done
  41.0 0.0 copy-start.5
  41.0 0.0 copy-start.4
  41.0 0.5 convolution_convert_fusion.2
  41.5 0.1 reshape_squeeze.13
  41.6 2.0 convolution_convert_fusion.3
  43.6 0.1 reshape_squeeze.12
  43.7 0.1 reshape_squeeze.15
  43.8 0.1 reshape_squeeze.14
  43.8 0.0 copy-done.5
  43.8 0.6 fusion.29
  44.4 0.7 iota_compare_fusion.1
  45.1 0.7 iota_compare_fusion
  45.8 0.0 copy-done.4
  45.8 149.7 %all-gather.4.cloned.1.call-done = bf16[5120,1280]{1,0:T(8,128)(2,1)} async-done(((bf16[640,1280]{1,0:T(8,128)(2,1)}), bf16[5120,1280]{1,0:T(8,128)(2,1)}) %all-gather.4.cloned.1.call-update) | async-done | bytes 13107216 | tf_op jit(solution)/shard_map/all_gather | solution.py:18
  195.5 12.6 %convolution_convert_fusion.1 = bf16[512,1280]{1,0:T(8,128)(2,1)S(1)} fusion(bf16[512,5120]{1,0:T(8,128)(2,1)} %param.8, bf16[5120,1280]{1,0:T(8,128)(2,1)} %all-gather.4.cloned.1.call-done), kind=kOutput, calls=%fused_computation.7 | convolution fusion | flops 6711541760 | bytes 19660800 | tf_op jit(solution)/shard_map/dot_general | solution.py:11
  208.2 2.1 gather_fusion
  210.3 1.5 copy.27
  211.8 1.6 convolution_multiply_fusion.1
  213.4 0.2 fusion.30
  213.6 2.0 fusion.7
  215.6 3.2 copy.32
  218.8 2.1 gather_fusion.1
  221.0 0.7 copy.33
  221.6 0.3 convolution_multiply_fusion
  221.9 0.2 fusion.31
  222.1 2.0 fusion.6
  224.1 0.0 copy-start.2
  224.1 3.4 copy.37
  227.5 0.0 copy-done.2
  227.5 7.2 %scatter_custom_fusion = f32[512,1280]{1,0:T(8,128)} fusion(s32[512]{0:T(512)S(1)} %bitcast.39, f32[]{:T(128)} %constant.5.clone.1, f32[512,1280]{1,0:T(8,128)S(1)} %copy-done.2, pred[512]{0:T(512)(128)(4,1)S(1)} %iota_compare_fusion.1), kind=kCustom, calls=%fused_computation.21 | custom fusion | flops 1310720 | bytes 5244416 | tf_op jit(solution)/shard_map/scatter-add | solution.py:50
  234.7 9.8 %scatter_custom_fusion.1 = f32[512,1280]{1,0:T(8,128)} fusion(f32[512,1280]{1,0:T(8,128)} %scatter_custom_fusion, s32[512]{0:T(512)S(1)} %bitcast.37, f32[512,1280]{1,0:T(8,128)} %copy.37, f32[]{:T(128)} %constant.5.clone.1, pred[512]{0:T(512)(128)(4,1)S(1)} %iota_compare_fusion), kind=kCustom, calls=%fused_computation.8 | custom fusion | flops 1310720 | bytes 5243904 | tf_op jit(solution)/shard_map/scatter-add | solution.py:50
  244.5 2.9 convert_element_type.60
  247.4 0.0 all-gather.6.cloned.1.call-update
  247.4 131.3 %all-gather.8.cloned.1.call-done = bf16[5120,1280]{1,0:T(8,128)(2,1)} async-done(((bf16[640,1280]{1,0:T(8,128)(2,1)}), bf16[5120,1280]{1,0:T(8,128)(2,1)}) %all-gather.8.cloned.1.call-update) | async-done | bytes 13107216 | tf_op jit(solution)/shard_map/all_gather | solution.py:53
  378.8 40.2 %all-gather.6.cloned.1.call-done = bf16[512,5120]{1,0:T(8,128)(2,1)} async-done(((bf16[512,1280]{1,0:T(8,128)(2,1)}), bf16[512,5120]{1,0:T(8,128)(2,1)}) %all-gather.6.cloned.1.call-update) | async-done | bytes 5242896 | tf_op jit(solution)/shard_map/all_gather | solution.py:52
  419.0 0.0 copy-start.1
  419.0 13.6 %convolution_convert_fusion = bf16[512,1280]{1,0:T(8,128)(2,1)} fusion(bf16[512,5120]{1,0:T(8,128)(2,1)} %all-gather.6.cloned.1.call-done, bf16[5120,1280]{1,0:T(8,128)(2,1)} %all-gather.8.cloned.1.call-done), kind=kOutput, calls=%fused_computation.6 | convolution fusion | flops 6711541760 | bytes 19660800 | tf_op jit(solution)/shard_map/dot_general | solution.py:11
  432.6 0.0 copy-done.1
  (6 shorter events, 0.1 us)
Async XLA Ops:
  6.5 34.5 %copy-start = (bf16[768,1280]{1,0:T(8,128)(2,1)S(1)}, bf16[768,1280]{1,0:T(8,128)(2,1)}, u32[]{:S(2)}) copy-start(bf16[768,1280]{1,0:T(8,128)(2,1)} %param.12) | copy-start | bytes 5898244
  6.5 1.5 copy-start.3
  6.5 189.0 %all-gather.4.cloned.1.call-start = ((), (), s32[]{:S(2)}) async-start(), calls=%async_computation | async-start | bytes 14745600 | tf_op jit(solution)/shard_map/all_gather | solution.py:18
  7.3 371.5 %all-gather.8.cloned.1.call-start = ((), (), s32[]{:S(2)}) async-start(), calls=%async_computation.2 | async-start | bytes 14745600 | tf_op jit(solution)/shard_map/all_gather | solution.py:53
  8.0 411.0 %all-gather.6.cloned.1.call-start = ((), (), s32[]{:S(2)}) async-start(), calls=%async_computation.1 | async-start | bytes 6553600 | tf_op jit(solution)/shard_map/all_gather | solution.py:52
  41.0 2.8 copy-start.5
  41.0 4.8 %copy-start.4 = (s32[2,512]{1,0:T(2,128)S(1)}, s32[2,512]{1,0:T(2,128)}, u32[]{:S(2)}) copy-start(s32[2,512]{1,0:T(2,128)} %param.14) | copy-start | bytes 12292
  224.1 3.4 copy-start.2
  419.0 13.6 %copy-start.1 = (bf16[768,1280]{1,0:T(8,128)(2,1)S(1)}, bf16[768,1280]{1,0:T(8,128)(2,1)}, u32[]{:S(2)}) copy-start(bf16[768,1280]{1,0:T(8,128)(2,1)} %param.12) | copy-start | bytes 5898244
Sparse Core Ops, SparseCore 0:
  9.6 185.9 all-gather.3
  197.7 180.9 all-gather.7
  380.3 38.6 all-gather.5
where the time goes:
time: 439 us
  waiting for transfers between devices  323 us (74%)
  matrix products  34.7 us (8%)
  blocking collectives  32.9 us (7%)
  other arithmetic  21.6 us (5%)
  local copies, waits for them, and re-layouts  13.9 us (3%)
  between operations  13.3 us (3%)
    all_gather x1, waiting for transfers between devices, shards(): lax.all_gather(w_query, 'ctx', axis=0, tiled=True)  150 us
    all_gather x1, waiting for transfers between devices, shards(): lax.all_gather(w_output, 'ctx', axis=0, tiled=True)  131 us
    all_gather x1, waiting for transfers between devices, shards(): all_heads = lax.all_gather(attended, 'head', axis=1, tiled=True)  40.2 us
    all_gather x1, blocking collectives, shards(): whole_audio = lax.all_gather(audio_tokens, 'ctx', axis=1, tiled=True)  32.9 us
    dot_general x2, matrix products, add_rows(): return jnp.dot(left_rows, shard_piece, preferred_element_type=jnp.float32)  26.2 us
    scatter-add x2, other arithmetic, shards(): summed = summed.at[target].add(blended)  17 us
  transfers between devices with their start and end apart: 3, of which 3 were waited for; matrix products, arithmetic and copies ran while one was open for 13% of the time, Pallas kernels for 0%

commit v1 on v0

--- a/solution.py
+++ b/solution.py
@@ -18,7 +18,17 @@
     queries = add_rows(video_rows, lax.all_gather(w_query, "ctx", axis=0, tiled=True)).astype(
         jnp.bfloat16
     )
-    whole_audio = lax.all_gather(audio_tokens, "ctx", axis=1, tiled=True)
+    n_blocks = lax.psum(1, "ctx")
+    p_next = sorted(((m, (m + 1) % n_blocks) for m in range(n_blocks)))
+    then = audio_tokens
+    shelf = [then]
+    for kk in range(1, n_blocks):
+        then = lax.ppermute(then, "ctx", p_next)
+        shelf.insert(0, then)
+    n_now = jnp.concatenate(shelf, 1)
+    inter = lax.axis_index("ctx")
+    block_out = inter + 1
+    whole_audio = jnp.roll(n_now, block_out * audio_tokens.shape[1], 1)
     key_rows = jnp.einsum(
         "sta,ad->std", whole_audio, w_key, preferred_element_type=jnp.float32
     ).astype(jnp.bfloat16)

time: 439 us -> 440 us (level)
  waiting for transfers between devices: 323 us -> 356 us
  blocking collectives: 32.9 us -> 0 us
    ppermute x0 -> x7, waiting for transfers between devices: none -> 42.7 us  [shards(): then = lax.ppermute(then, 'ctx', p_next)]
    all_gather x1 -> x0, blocking collectives: 32.9 us -> none  [shards(): whole_audio = lax.all_gather(audio_tokens, 'ctx', axis=1, tiled=True)]
    all_gather x1, waiting for transfers between devices: 150 us -> 138 us  [shards(): lax.all_gather(w_query, 'ctx', axis=0, tiled=True)]
  transfers between devices with their start and end apart: 3 -> 10, of which waited for: 3 -> 10; matrix products, arithmetic and copies ran while one was open for 13% -> 12% of each run, Pallas kernels for 0% -> 0%
where the time goes in v1:
time: 440 us
  waiting for transfers between devices  356 us (81%)
  matrix products  33.2 us (8%)
  other arithmetic  21.8 us (5%)
  between operations  13.3 us (3%)
  local copies, waits for them, and re-layouts  12.8 us (3%)
    all_gather x1, waiting for transfers between devices, shards(): lax.all_gather(w_query, 'ctx', axis=0, tiled=True)  138 us
    all_gather x1, waiting for transfers between devices, shards(): lax.all_gather(w_output, 'ctx', axis=0, tiled=True)  134 us
    ppermute x7, waiting for transfers between devices, shards(): then = lax.ppermute(then, 'ctx', p_next)  42.7 us
    all_gather x1, waiting for transfers between devices, shards(): all_heads = lax.all_gather(attended, 'head', axis=1, tiled=True)  40.2 us
    dot_general x2, matrix products, add_rows(): return jnp.dot(left_rows, shard_piece, preferred_element_type=jnp.float32)  26.2 us
    scatter-add x2, other arithmetic, shards(): summed = summed.at[target].add(blended)  17.2 us
  transfers between devices with their start and end apart: 10, of which 10 were waited for; matrix products, arithmetic and copies ran while one was open for 12% of the time, Pallas kernels for 0%

profile of v1, /device:TPU:0, one launch (start us, length us, event | category | flops | bytes accessed | tf_op | source)
XLA Modules:
  0.0 439.8 jit_solution(13393725382631965448)
XLA Ops:
  6.5 0.0 copy-start
  6.5 0.0 copy-start.3
  6.5 0.0 copy-start.4
  6.5 0.0 copy-start.5
  6.5 0.0 all-gather.4.cloned.1.call-start
  6.6 0.7 all-gather.4.cloned.1.call-update
  7.3 0.0 all-gather.8.cloned.1.call-start
  7.3 0.7 all-gather.8.cloned.1.call-update
  8.0 0.0 all-gather.6.cloned.1.call-start
  8.1 0.0 copy-done.3
  8.1 3.0 collective-permute-start
  11.1 4.7 %collective-permute-done = bf16[2,4,768]{2,1,0:T(4,128)(2,1)S(1)} collective-permute-done((bf16[2,4,768]{2,1,0:T(4,128)(2,1)S(1)}, bf16[2,4,768]{2,1,0:T(4,128)(2,1)S(1)}, u32[]{:S(2)}, u32[]{:S(2)}) %collective-permute-start) | collective-permute-done | bytes 12320 | tf_op jit(solution)/shard_map/ppermute | solution.py:26
  15.8 0.0 collective-permute-start.1
  15.8 0.0 copy-done.4
  15.8 6.4 %collective-permute-done.1 = bf16[2,4,768]{2,1,0:T(4,128)(2,1)S(1)} collective-permute-done((bf16[2,4,768]{2,1,0:T(4,128)(2,1)S(1)}, bf16[2,4,768]{2,1,0:T(4,128)(2,1)S(1)}, u32[]{:S(2)}, u32[]{:S(2)}) %collective-permute-start.1) | collective-permute-done | bytes 12320 | tf_op jit(solution)/shard_map/ppermute | solution.py:26
  22.2 0.0 collective-permute-start.2
  22.2 0.0 copy-done.5
  22.2 0.6 fusion.31
  22.8 6.0 %collective-permute-done.2 = bf16[2,4,768]{2,1,0:T(4,128)(2,1)S(1)} collective-permute-done((bf16[2,4,768]{2,1,0:T(4,128)(2,1)S(1)}, bf16[2,4,768]{2,1,0:T(4,128)(2,1)S(1)}, u32[]{:S(2)}, u32[]{:S(2)}) %collective-permute-start.2) | collective-permute-done | bytes 12320 | tf_op jit(solution)/shard_map/ppermute | solution.py:26
  28.7 0.0 collective-permute-start.3
  28.8 6.7 %collective-permute-done.3 = bf16[2,4,768]{2,1,0:T(4,128)(2,1)S(1)} collective-permute-done((bf16[2,4,768]{2,1,0:T(4,128)(2,1)S(1)}, bf16[2,4,768]{2,1,0:T(4,128)(2,1)S(1)}, u32[]{:S(2)}, u32[]{:S(2)}) %collective-permute-start.3) | collective-permute-done | bytes 12320 | tf_op jit(solution)/shard_map/ppermute | solution.py:26
  35.5 0.0 collective-permute-start.4
  35.5 6.8 %collective-permute-done.4 = bf16[2,4,768]{2,1,0:T(4,128)(2,1)S(1)} collective-permute-done((bf16[2,4,768]{2,1,0:T(4,128)(2,1)S(1)}, bf16[2,4,768]{2,1,0:T(4,128)(2,1)S(1)}, u32[]{:S(2)}, u32[]{:S(2)}) %collective-permute-start.4) | collective-permute-done | bytes 12320 | tf_op jit(solution)/shard_map/ppermute | solution.py:26
  42.3 0.0 collective-permute-start.5
  42.3 0.6 iota_compare_fusion.1
  43.0 6.0 %collective-permute-done.5 = bf16[2,4,768]{2,1,0:T(4,128)(2,1)S(1)} collective-permute-done((bf16[2,4,768]{2,1,0:T(4,128)(2,1)S(1)}, bf16[2,4,768]{2,1,0:T(4,128)(2,1)S(1)}, u32[]{:S(2)}, u32[]{:S(2)}) %collective-permute-start.5) | collective-permute-done | bytes 12320 | tf_op jit(solution)/shard_map/ppermute | solution.py:26
  49.0 0.0 collective-permute-start.6
  49.0 0.7 iota_compare_fusion
  49.7 6.0 %collective-permute-done.6 = bf16[2,4,768]{2,1,0:T(4,128)(2,1)S(1)} collective-permute-done((bf16[2,4,768]{2,1,0:T(4,128)(2,1)S(1)}, bf16[2,4,768]{2,1,0:T(4,128)(2,1)S(1)}, u32[]{:S(2)}, u32[]{:S(2)}) %collective-permute-start.6) | collective-permute-done | bytes 12320 | tf_op jit(solution)/shard_map/ppermute | solution.py:26
  55.7 0.2 concatenate.6
  55.9 0.0 copy-done
  56.0 0.5 convolution_convert_fusion.2
  56.4 0.1 reshape_squeeze.15
  56.5 2.0 convolution_convert_fusion.3
  58.5 0.1 reshape_squeeze.14
  58.6 0.1 reshape_squeeze.13
  58.7 0.1 reshape_squeeze.12
  58.7 137.5 %all-gather.4.cloned.1.call-done = bf16[5120,1280]{1,0:T(8,128)(2,1)} async-done(((bf16[640,1280]{1,0:T(8,128)(2,1)}), bf16[5120,1280]{1,0:T(8,128)(2,1)}) %all-gather.4.cloned.1.call-update) | async-done | bytes 13107216 | tf_op jit(solution)/shard_map/all_gather | solution.py:18
  196.3 12.6 %convolution_convert_fusion.1 = bf16[512,1280]{1,0:T(8,128)(2,1)S(1)} fusion(bf16[512,5120]{1,0:T(8,128)(2,1)} %param.8, bf16[5120,1280]{1,0:T(8,128)(2,1)} %all-gather.4.cloned.1.call-done), kind=kOutput, calls=%fused_computation.7 | convolution fusion | flops 6711541760 | bytes 19660800 | tf_op jit(solution)/shard_map/dot_general | solution.py:11
  208.9 2.1 gather_fusion.1
  211.0 1.5 copy.20
  212.5 1.6 convolution_multiply_fusion
  214.1 0.2 fusion.33
  214.3 2.1 fusion.6
  216.4 3.2 copy.24
  219.6 2.1 gather_fusion
  221.7 0.7 copy.15
  222.4 0.3 convolution_multiply_fusion.1
  222.7 0.2 fusion.32
  222.9 0.6 fusion.7
  223.5 2.1 copy.19
  225.6 0.0 copy-start.2
  225.6 8.6 %scatter_custom_fusion = f32[512,1280]{1,0:T(8,128)} fusion(s32[512]{0:T(512)S(1)} %bitcast.39, f32[]{:T(128)} %constant.30.clone.1, f32[512,1280]{1,0:T(8,128)} %copy.19, pred[512]{0:T(512)(128)(4,1)S(1)} %iota_compare_fusion.1), kind=kCustom, calls=%fused_computation.21 | custom fusion | flops 1310720 | bytes 5244416 | tf_op jit(solution)/shard_map/scatter-add | solution.py:60
  234.1 0.0 copy-done.2
  234.1 8.6 %scatter_custom_fusion.1 = f32[512,1280]{1,0:T(8,128)} fusion(f32[512,1280]{1,0:T(8,128)} %scatter_custom_fusion, s32[512]{0:T(512)S(1)} %bitcast.37, f32[512,1280]{1,0:T(8,128)S(1)} %copy-done.2, f32[]{:T(128)} %constant.30.clone.1, pred[512]{0:T(512)(128)(4,1)S(1)} %iota_compare_fusion), kind=kCustom, calls=%fused_computation.8 | custom fusion | flops 1310720 | bytes 5243904 | tf_op jit(solution)/shard_map/scatter-add | solution.py:60
  242.8 3.0 convert_element_type.60
  245.7 0.0 all-gather.6.cloned.1.call-update
  245.7 133.7 %all-gather.8.cloned.1.call-done = bf16[5120,1280]{1,0:T(8,128)(2,1)} async-done(((bf16[640,1280]{1,0:T(8,128)(2,1)}), bf16[5120,1280]{1,0:T(8,128)(2,1)}) %all-gather.8.cloned.1.call-update) | async-done | bytes 13107216 | tf_op jit(solution)/shard_map/all_gather | solution.py:63
  379.5 40.2 %all-gather.6.cloned.1.call-done = bf16[512,5120]{1,0:T(8,128)(2,1)} async-done(((bf16[512,1280]{1,0:T(8,128)(2,1)}), bf16[512,5120]{1,0:T(8,128)(2,1)}) %all-gather.6.cloned.1.call-update) | async-done | bytes 5242896 | tf_op jit(solution)/shard_map/all_gather | solution.py:62
  419.7 0.0 copy-start.1
  419.7 13.6 %convolution_convert_fusion = bf16[512,1280]{1,0:T(8,128)(2,1)} fusion(bf16[512,5120]{1,0:T(8,128)(2,1)} %all-gather.6.cloned.1.call-done, bf16[5120,1280]{1,0:T(8,128)(2,1)} %all-gather.8.cloned.1.call-done), kind=kOutput, calls=%fused_computation.6 | convolution fusion | flops 6711541760 | bytes 19660800 | tf_op jit(solution)/shard_map/dot_general | solution.py:11
  433.3 0.0 copy-done.1
  (5 shorter events, 0.0 us)
Async XLA Ops:
  6.5 49.4 %copy-start = (bf16[768,1280]{1,0:T(8,128)(2,1)S(1)}, bf16[768,1280]{1,0:T(8,128)(2,1)}, u32[]{:S(2)}) copy-start(bf16[768,1280]{1,0:T(8,128)(2,1)} %param.12) | copy-start | bytes 5898244
  6.5 1.5 copy-start.3
  6.5 9.2 %copy-start.4 = (s32[2,512]{1,0:T(2,128)S(1)}, s32[2,512]{1,0:T(2,128)}, u32[]{:S(2)}) copy-start(s32[2,512]{1,0:T(2,128)} %param.14) | copy-start | bytes 12292
  6.5 15.6 %copy-start.5 = (s32[2,1]{0,1:T(1,128)S(1)}, s32[2,1]{0,1:T(1,128)}, u32[]{:S(2)}) copy-start(s32[2,1]{0,1:T(1,128)} %param.15) | copy-start | bytes 28
  6.5 189.7 %all-gather.4.cloned.1.call-start = ((), (), s32[]{:S(2)}) async-start(), calls=%async_computation | async-start | bytes 14745600 | tf_op jit(solution)/shard_map/all_gather | solution.py:18
  7.3 372.2 %all-gather.8.cloned.1.call-start = ((), (), s32[]{:S(2)}) async-start(), calls=%async_computation.2 | async-start | bytes 14745600 | tf_op jit(solution)/shard_map/all_gather | solution.py:63
  8.0 411.7 %all-gather.6.cloned.1.call-start = ((), (), s32[]{:S(2)}) async-start(), calls=%async_computation.1 | async-start | bytes 6553600 | tf_op jit(solution)/shard_map/all_gather | solution.py:62
  8.1 7.7 %collective-permute-start = (bf16[2,4,768]{2,1,0:T(4,128)(2,1)S(1)}, bf16[2,4,768]{2,1,0:T(4,128)(2,1)S(1)}, u32[]{:S(2)}, u32[]{:S(2)}) collective-permute-start(bf16[2,4,768]{2,1,0:T(4,128)(2,1)S(1)} %copy-done.3), channel_id=1, source_target_pairs={{0,4},{4,8},{8,12},{12,16},{16,20},{20,24},{24,28},{28,0},{1,5},{5... | collective-permute-start | bytes 36872 | tf_op jit(solution)/shard_map/ppermute | solution.py:26
  15.8 6.4 %collective-permute-start.1 = (bf16[2,4,768]{2,1,0:T(4,128)(2,1)S(1)}, bf16[2,4,768]{2,1,0:T(4,128)(2,1)S(1)}, u32[]{:S(2)}, u32[]{:S(2)}) collective-permute-start(bf16[2,4,768]{2,1,0:T(4,128)(2,1)S(1)} %collective-permute-done), channel_id=1, source_target_pairs={{0,4},{4,8},{8,12},{12,16},{16,20},{20,24},{24,28},{28,0},{1,5},{5... | collective-permute-start | bytes 36872 | tf_op jit(solution)/shard_map/ppermute | solution.py:26
  22.2 6.6 %collective-permute-start.2 = (bf16[2,4,768]{2,1,0:T(4,128)(2,1)S(1)}, bf16[2,4,768]{2,1,0:T(4,128)(2,1)S(1)}, u32[]{:S(2)}, u32[]{:S(2)}) collective-permute-start(bf16[2,4,768]{2,1,0:T(4,128)(2,1)S(1)} %collective-permute-done.1), channel_id=1, source_target_pairs={{0,4},{4,8},{8,12},{12,16},{16,20},{20,24},{24,28},{28,0},{1,5},{5... | collective-permute-start | bytes 36872 | tf_op jit(solution)/shard_map/ppermute | solution.py:26
  28.7 6.7 %collective-permute-start.3 = (bf16[2,4,768]{2,1,0:T(4,128)(2,1)S(1)}, bf16[2,4,768]{2,1,0:T(4,128)(2,1)S(1)}, u32[]{:S(2)}, u32[]{:S(2)}) collective-permute-start(bf16[2,4,768]{2,1,0:T(4,128)(2,1)S(1)} %collective-permute-done.2), channel_id=1, source_target_pairs={{0,4},{4,8},{8,12},{12,16},{16,20},{20,24},{24,28},{28,0},{1,5},{5... | collective-permute-start | bytes 36872 | tf_op jit(solution)/shard_map/ppermute | solution.py:26
  35.5 6.8 %collective-permute-start.4 = (bf16[2,4,768]{2,1,0:T(4,128)(2,1)S(1)}, bf16[2,4,768]{2,1,0:T(4,128)(2,1)S(1)}, u32[]{:S(2)}, u32[]{:S(2)}) collective-permute-start(bf16[2,4,768]{2,1,0:T(4,128)(2,1)S(1)} %collective-permute-done.3), channel_id=1, source_target_pairs={{0,4},{4,8},{8,12},{12,16},{16,20},{20,24},{24,28},{28,0},{1,5},{5... | collective-permute-start | bytes 36872 | tf_op jit(solution)/shard_map/ppermute | solution.py:26
  42.3 6.7 %collective-permute-start.5 = (bf16[2,4,768]{2,1,0:T(4,128)(2,1)S(1)}, bf16[2,4,768]{2,1,0:T(4,128)(2,1)S(1)}, u32[]{:S(2)}, u32[]{:S(2)}) collective-permute-start(bf16[2,4,768]{2,1,0:T(4,128)(2,1)S(1)} %collective-permute-done.4), channel_id=1, source_target_pairs={{0,4},{4,8},{8,12},{12,16},{16,20},{20,24},{24,28},{28,0},{1,5},{5... | collective-permute-start | bytes 36872 | tf_op jit(solution)/shard_map/ppermute | solution.py:26
  49.0 6.7 %collective-permute-start.6 = (bf16[2,4,768]{2,1,0:T(4,128)(2,1)S(1)}, bf16[2,4,768]{2,1,0:T(4,128)(2,1)S(1)}, u32[]{:S(2)}, u32[]{:S(2)}) collective-permute-start(bf16[2,4,768]{2,1,0:T(4,128)(2,1)S(1)} %collective-permute-done.5), channel_id=1, source_target_pairs={{0,4},{4,8},{8,12},{12,16},{16,20},{20,24},{24,28},{28,0},{1,5},{5... | collective-permute-start | bytes 36872 | tf_op jit(solution)/shard_map/ppermute | solution.py:26
  225.6 8.6 %copy-start.2 = (f32[512,1280]{1,0:T(8,128)S(1)}, f32[512,1280]{1,0:T(8,128)}, u32[]{:S(2)}) copy-start(f32[512,1280]{1,0:T(8,128)} %copy.24) | copy-start | bytes 7864324
  419.7 13.6 %copy-start.1 = (bf16[768,1280]{1,0:T(8,128)(2,1)S(1)}, bf16[768,1280]{1,0:T(8,128)(2,1)}, u32[]{:S(2)}) copy-start(bf16[768,1280]{1,0:T(8,128)(2,1)} %param.12) | copy-start | bytes 5898244
Sparse Core Ops, SparseCore 0:
  9.6 186.6 all-gather.3
  198.4 180.9 all-gather.7
  381.1 38.6 all-gather.5
